TPU v7x, 128 devices: a whole 4x4x4 slice. The times are simulated.
128 devices in a mesh: ctx: 32 (over z, x, core), exp: 4 (over y).
Axes of the slice: x: 4, y: 4, z: 4, core: 2. Of those that a mesh axis runs over, the one named last changes fastest.
Arguments:
- queries: bfloat16 [16384, 6144], P('ctx', 'exp'), may hold values from -0.52734375 to 0.52734375
- key_vectors: bfloat16 [16384, 6144], P('ctx', 'exp'), may hold values from -6 to 6
- values: bfloat16 [16384, 6144], P('ctx', 'exp'), may hold values from -6 to 6
- log_decay: float32 [16384, 48], P('ctx', 'exp'), may hold values from -1 to 0, as said below
- out_gate: bfloat16 [16384, 6144], P(('ctx', 'exp')), may hold values from -6 to 6
- residual: bfloat16 [16384, 6144], P(('ctx', 'exp')), may hold values from -6 to 6
- attn_gain: float32 [6144], replicated, may hold values from 0.1 to 1.9
- moe_gain: float32 [6144], replicated, may hold values from 0.1 to 1.9
- expert_ids: int32 [16384, 2], P(('ctx', 'exp')), may hold values from 0 to 31, as said below
- route_weights: float32 [16384, 2], P(('ctx', 'exp')), may hold values from 0.5 to 1.5
- w_gate: bfloat16 [4, 6144, 9216], P('exp', None, 'ctx'), may hold values from -0.078125 to 0.078125
- w_up: bfloat16 [4, 6144, 9216], P('exp', None, 'ctx'), may hold values from -0.078125 to 0.078125
- w_down: bfloat16 [4, 9216, 6144], P('exp', 'ctx'), may hold values from -0.0625 to 0.0625
Outputs:
- hidden: bfloat16 [16384, 6144], P(('ctx', 'exp'))
- moe_out: bfloat16 [16384, 6144], P(('ctx', 'exp'))
Inputs may be any that keep to these rules, and one draw needn't show every extreme that they name: `expert_ids`: each token names two different experts, at most one of them below 4. The 128 rows of one device name each expert below 4 at most 4 times; in every draw one expert is named exactly 4 times by every device of some index of ctx. `log_decay`: every entry is negative.
All inputs are finite; a program needn't handle non-finite values.
Results may differ from a plain program's by a relative error of at most 0.03.
Values may be sent and summed in bfloat16 or wider, within the bound.
No kernel may reach another device: no remote copies, remote signals or barrier semaphores. Data moves between devices by JAX's collectives and lax.ppermute only.
A program may use at most 128 MiB of HBM per device.

v0:
```python
import jax
import jax.numpy as jnp
from jax import lax
from jax.sharding import PartitionSpec as P

HEAD_DIM = 128
CAP = 4


def entering(shard, axis, combine, identity):
    peers, place = (lax.axis_size(axis), lax.axis_index(axis))
    everything = jax.tree.map(
        lambda part, kind: lax.all_gather(part.astype(kind), axis),
        shard,
        (jnp.bfloat16, jnp.bfloat16),
    )
    start = jax.tree.map(
        lambda part, zero: jnp.broadcast_to(jnp.asarray(zero, part.dtype), part.shape),
        shard,
        identity,
    )

    def turn(k, before):
        reached = k < place
        new = combine(
            before, jax.tree.map(lambda part, own: part[k].astype(own.dtype), everything, shard)
        )
        return jax.tree.map(lambda a, b: jnp.where(reached, a, b), new, before)

    return lax.fori_loop(0, peers, turn, start)


def combine_states(earlier, later):
    return (earlier[0] * later[0], later[0][:, None, None] * earlier[1] + later[1])


def local(
    queries,
    key_vectors,
    values,
    log_decay,
    out_gate,
    residual,
    attn_gain,
    moe_gain,
    expert_ids,
    route_weights,
    w_gate,
    w_up,
    w_down,
):
    highest = lax.Precision.HIGHEST
    row_total = queries.shape[0]
    head_count = log_decay.shape[1]
    query_heads = queries.reshape(row_total, head_count, HEAD_DIM)
    key_heads = key_vectors.reshape(row_total, head_count, HEAD_DIM)
    value_heads = values.reshape(row_total, head_count, HEAD_DIM)
    cumulative = jnp.cumsum(log_decay, axis=0)
    final_cum = cumulative[-1]
    weighted_keys = (
        key_heads.astype(jnp.float32) * jnp.exp(final_cum[None, :] - cumulative)[:, :, None]
    )
    local_state = jnp.einsum(
        "shd,she->hde", weighted_keys, value_heads.astype(jnp.float32), precision=highest
    )
    block_decay = jnp.exp(final_cum)
    prior = entering(
        (block_decay, local_state),
        "ctx",
        combine_states,
        (jnp.ones_like(block_decay), jnp.zeros_like(local_state)),
    )
    carried = prior[1]
    block_size = min(512, row_total)

    def query_part(block_index):
        offset = block_index * block_size
        scores = jnp.einsum(
            "thd,shd->hts", query_heads, key_heads, preferred_element_type=jnp.float32
        )
        log_gap = cumulative.T[:, :, None] - cumulative.T[:, None, :]
        causal = (offset + jnp.arange(block_size))[:, None] >= jnp.arange(row_total)[None, :]
        decay_now = jnp.where(causal[None], jnp.exp(jnp.minimum(log_gap, 0.0)), 0.0)
        weights = (scores * decay_now).astype(jnp.bfloat16)
        inside = jnp.einsum(
            "hts,shd->thd", weights, value_heads, preferred_element_type=jnp.float32
        )
        scaled = query_heads.astype(jnp.float32) * jnp.exp(cumulative)[:, :, None]
        carried_part = jnp.einsum("thd,hde->the", scaled, carried, precision=highest)
        return (inside + carried_part).astype(jnp.bfloat16)

    blocks_out = lax.map(query_part, jnp.arange(row_total // block_size))
    attention = blocks_out.reshape(row_total, head_count * HEAD_DIM)
    token_rows = lax.all_to_all(attention, "exp", split_axis=0, concat_axis=1, tiled=True)
    attn_f32 = token_rows.astype(jnp.float32)
    attn_norm = (
        attn_f32
        * lax.rsqrt(jnp.mean(attn_f32 * attn_f32, axis=-1, keepdims=True) + 1e-05)
        * attn_gain
    )
    hidden = (
        residual.astype(jnp.float32) + attn_norm * jax.nn.sigmoid(out_gate.astype(jnp.float32))
    ).astype(jnp.bfloat16)
    hidden_f32 = hidden.astype(jnp.float32)
    normed = (
        hidden_f32
        * lax.rsqrt(jnp.mean(hidden_f32 * hidden_f32, axis=-1, keepdims=True) + 1e-05)
        * moe_gain
    ).astype(jnp.bfloat16)
    held_count = lax.axis_size("exp")
    expert_index = jnp.arange(held_count, dtype=jnp.int32)
    naming = expert_ids[:, :, None] == expert_index[None, None, :]
    member = jnp.any(naming, axis=1)
    slot_rank = jnp.cumsum(member.astype(jnp.int32), axis=0) - 1
    slot_index = jnp.arange(CAP, dtype=jnp.int32)
    placing = (
        member.T[:, None, :] & (slot_rank.T[:, None, :] == slot_index[None, :, None])
    ).astype(jnp.bfloat16)
    outgoing = jnp.einsum(
        "jct,td->jcd", placing, normed, preferred_element_type=jnp.float32
    ).astype(jnp.bfloat16)
    incoming = lax.all_to_all(outgoing, "exp", split_axis=0, concat_axis=0, tiled=True)
    flat_rows = incoming.reshape(held_count * CAP, incoming.shape[2])
    gate_matrix = w_gate[0]
    up_matrix = w_up[0]
    down_matrix = w_down[0]
    pieces = lax.all_gather(flat_rows, "ctx", axis=0, tiled=True)
    gate_part = jnp.dot(pieces, gate_matrix, preferred_element_type=jnp.float32)
    up_part = jnp.dot(pieces, up_matrix, preferred_element_type=jnp.float32)
    activations = (jax.nn.silu(gate_part) * up_part).astype(jnp.bfloat16)
    summed = lax.psum_scatter(
        jnp.dot(activations, down_matrix, preferred_element_type=jnp.float32).astype(jnp.bfloat16),
        "ctx",
        scatter_dimension=0,
        tiled=True,
    ).astype(jnp.float32)
    leaving = summed.astype(jnp.bfloat16).reshape(held_count, CAP, summed.shape[1])
    returned = lax.all_to_all(leaving, "exp", split_axis=0, concat_axis=0, tiled=True)
    chosen = jnp.sum(jnp.where(expert_ids < held_count, route_weights, 0.0), axis=1)
    gathered_back = jnp.einsum("jct,jcd->td", placing, returned, preferred_element_type=jnp.float32)
    moe_out = (gathered_back * chosen[:, None]).astype(jnp.bfloat16)
    return (hidden, moe_out)


def solution(mesh):
    in_specs = (
        P("ctx", "exp"),
        P("ctx", "exp"),
        P("ctx", "exp"),
        P("ctx", "exp"),
        P(("ctx", "exp"), None),
        P(("ctx", "exp"), None),
        P(),
        P(),
        P(("ctx", "exp"), None),
        P(("ctx", "exp"), None),
        P("exp", None, "ctx"),
        P("exp", None, "ctx"),
        P("exp", "ctx", None),
    )
    out_specs = (P(("ctx", "exp"), None), P(("ctx", "exp"), None))
    return jax.shard_map(local, mesh=mesh, in_specs=in_specs, out_specs=out_specs, check_vma=False)
```

profile of v0, /device:TPU:0, one launch (start us, length us, event | category | flops | bytes accessed | tf_op | source)
XLA Modules:
  0.0 408.7 jit_solution(17558675305011067984)
XLA Ops:
  10.1 3.1 reduce-window.6
  15.9 2.6 copy.101
  18.5 2.6 copy.106
  22.4 4.3 %fusion.35 = bf16[12,128,128]{2,1,0:T(8,128)(2,1)} fusion(bf16[512,12,128]{0,2,1:T(8,128)(2,1)} %bitcast.85, bf16[512,12,128]{0,2,1:T(8,128)(2,1)} %bitcast.83, f32[512,12]{0,1:T(8,128)S(1)} %get-tuple-element.175), kind=kOutput, calls=%fused_computation.42 | convolution fusion | flops 1209729024 | bytes 3563520 | tf_op jit(solution)/shard_map/shd,she->hde/dot_general | solution.py:63
  27.7 22.8 %all-gather.1 = bf16[32,1,12]{2,1,0:T(2,128)(2,1)S(1)} all-gather(bf16[1,1,12]{2,1,0:T(2,128)(2,1)S(1)} %bitcast.98), channel_id=1, replica_groups=mesh['ctx'=32,'exp'=4] {'ctx'}, dimensions={0}, use_global_device_ids=true | all-gather | bytes 792 | tf_op jit(solution)/shard_map/all_gather | solution.py:13
  50.5 2.6 copy.100
  53.9 38.4 %all-gather.7.cloned.1.call-done = bf16[384,128,128]{2,1,0:T(8,128)(2,1)} async-done(((bf16[12,128,128]{2,1,0:T(8,128)(2,1)}), bf16[384,128,128]{2,1,0:T(8,128)(2,1)}) %all-gather.7.cloned.1.call-update) | async-done | bytes 12582928 | tf_op jit(solution)/shard_map/all_gather | solution.py:13
  92.4 72.8 %while.18 = (s32[]{:T(128)}, f32[12,128,128]{2,1,0:T(8,128)}, s32[]{:T(128)}, bf16[32,12]{1,0:T(8,128)(2,1)S(1)}, bf16[32,12,128,128]{3,2,1,0:T(8,128)(2,1)}, /*index=5*/s32[]{:T(128)}, s32[]{:T(128)}) while((s32[]{:T(128)}, f32[12,128,128]{2,1,0:T(8,128)}, s32[]{:T(128)}, bf16[32,12]{1,0:T(8,128)(2,1)S(1)}, ...), condition=%wide.region_3.4_spmd.clone, body=%wide.region_2.3_spmd.clone.sunk | while | flops 983056 | bytes 1966305 | solution.py:30
  165.1 8.3 %fusion.20 = f32[12,128,512]{1,2,0:T(8,128)} fusion(f32[12,128,128]{2,1,0:T(8,128)} %get-tuple-element.117, bf16[512,12,128]{0,2,1:T(8,128)(2,1)} %bitcast.87, f32[512,12]{0,1:T(8,128)} %get-tuple-element.174), kind=kOutput, calls=%fused_computation.30 | convolution fusion | flops 1209532416 | bytes 5529600 | tf_op jit(solution)/shard_map/while/body/eval_jaxpr/thd,hde->the/dot_general | solution.py:89
  173.4 8.8 %fusion.19 = bf16[512,12,128]{2,0,1:T(8,128)(2,1)} fusion(f32[12,128,512]{1,2,0:T(8,128)} %fusion.20, bf16[512,12,128]{0,2,1:T(8,128)(2,1)} %bitcast.86, f32[12,512]{1,0:T(8,128)} %bitcast.93, pred[512,512]{1,0:T(8,128)(4,1)} %iota_compare_fusion, bf16[512,12,128]{0,2,1:T(8,128)(2,1)} %bitcast.88, bf16[512,12,128]{0,2,1:T(8,128)(2,1)} %bitcast.84), kind=kOutput, calls=%fused_computation.28 | convolution fusion | flops 1627914240 | bytes 9723904 | tf_op jit(solution)/shard_map/while/body/eval_jaxpr/hts,shd->thd/dot_general | solution.py:85
  184.8 3.5 all_to_all.16
  188.3 2.8 copy.115
  191.1 4.3 %all-to-all-start = ((bf16[4,128,1536]{1,2,0:T(8,128)(2,1)}), bf16[4,128,1536]{1,2,0:T(8,128)(2,1)}, u32[]{:S(2)}, u32[]{:S(2)}) async-start(bf16[4,128,1536]{1,2,0:T(8,128)(2,1)} %copy.115), calls=%async_computation | async-start | bytes 3145728 | tf_op jit(solution)/shard_map/all_to_all | solution.py:94
  195.7 2.6 copy.116
  205.6 11.3 %all-to-all-done = bf16[4,128,1536]{1,2,0:T(8,128)(2,1)} async-done(((bf16[4,128,1536]{1,2,0:T(8,128)(2,1)}), bf16[4,128,1536]{1,2,0:T(8,128)(2,1)}, u32[]{:S(2)}, u32[]{:S(2)}) %all-to-all-start) | async-done | bytes 1572896 | tf_op jit(solution)/shard_map/all_to_all | solution.py:94
  219.1 3.2 fusion.12
  224.7 9.4 %all_to_all.23 = bf16[4,4,6144]{2,1,0:T(4,128)(2,1)} all-to-all(bf16[4,4,6144]{2,1,0:T(4,128)(2,1)S(1)} %convolution_convert_fusion.1), channel_id=1, replica_groups=mesh['ctx'=32,'exp'=4] {'exp'}, dimensions={0} | all-to-all | bytes 393216 | tf_op jit(solution)/shard_map/all_to_all | solution.py:122
  235.8 47.0 %all-gather.5.cloned.1.call-done = bf16[512,6144]{1,0:T(8,128)(2,1)} async-done(((bf16[16,6144]{1,0:T(8,128)(2,1)}), bf16[512,6144]{1,0:T(8,128)(2,1)}) %all-gather.5.cloned.1.call-update) | async-done | bytes 6291472 | tf_op jit(solution)/shard_map/all_gather | solution.py:127
  282.7 6.7 %fusion.10 = f32[512,288]{0,1:T(8,128)} fusion(bf16[512,6144]{1,0:T(8,128)(2,1)} %all-gather.5.cloned.1.call-done, bf16[1,6144,288]{1,2,0:T(8,128)(2,1)} %param.25), kind=kOutput, calls=%fused_computation.17 | convolution fusion | flops 1811939328 | bytes 10420224 | tf_op jit(solution)/shard_map/dot_general | solution.py:128
  289.4 12.1 %convolution_convert_fusion = bf16[512,6144]{1,0:T(8,128)(2,1)} fusion(bf16[1,288,6144]{2,1,0:T(8,128)(2,1)S(1)} %copy-done, bf16[512,6144]{1,0:T(8,128)(2,1)} %all-gather.5.cloned.1.call-done, bf16[1,6144,288]{1,2,0:T(8,128)(2,1)} %param.26, f32[512,288]{0,1:T(8,128)} %fusion.10), kind=kOutput, calls=%fused_computation.4 | convolution fusion | flops 3627909120 | bytes 20250624 | tf_op jit(solution)/shard_map/dot_general | solution.py:132
  301.5 85.5 %reduce-scatter.2.cloned.1.call-done = bf16[16,6144]{1,0:T(8,128)(2,1)} async-done(((bf16[512,6144]{1,0:T(8,128)(2,1)}), bf16[16,6144]{1,0:T(8,128)(2,1)}) %reduce-scatter.2.cloned.1.call-update) | async-done | bytes 196624 | tf_op jit(solution)/shard_map/reduce_scatter | solution.py:131
  388.6 4.3 %all-to-all-start.2 = ((bf16[4,4,6144]{2,1,0:T(4,128)(2,1)}), bf16[4,4,6144]{2,1,0:T(4,128)(2,1)}, u32[]{:S(2)}, u32[]{:S(2)}) async-start(bf16[4,4,6144]{2,1,0:T(4,128)(2,1)} %reshape.116), calls=%async_computation.3 | async-start | bytes 393216 | tf_op jit(solution)/shard_map/all_to_all | solution.py:138
  395.5 3.8 all-to-all-done.2
  399.3 2.8 fusion.2
  (114 shorter events, 102.0 us)
Async XLA Ops:
  7.2 282.2 %copy-start = (bf16[1,288,6144]{2,1,0:T(8,128)(2,1)S(1)}, bf16[1,288,6144]{2,1,0:T(8,128)(2,1)}, u32[]{:S(2)}) copy-start(bf16[1,288,6144]{2,1,0:T(8,128)(2,1)} %param.27) | copy-start | bytes 10616836
  7.2 85.2 %all-gather.7.cloned.1.call-start = ((), (), s32[]{:S(2)}) async-start(), calls=%async_computation.6 | async-start | bytes 12976128 | tf_op jit(solution)/shard_map/all_gather | solution.py:13
  15.1 0.6 copy-start.2
  191.1 25.8 %all-to-all-start = ((bf16[4,128,1536]{1,2,0:T(8,128)(2,1)}), bf16[4,128,1536]{1,2,0:T(8,128)(2,1)}, u32[]{:S(2)}, u32[]{:S(2)}) async-start(bf16[4,128,1536]{1,2,0:T(8,128)(2,1)} %copy.115), calls=%async_computation | async-start | bytes 3145728 | tf_op jit(solution)/shard_map/all_to_all | solution.py:94
  195.4 5.4 %copy-start.3 = (s32[128,2]{0,1:T(2,128)S(1)}, s32[128,2]{0,1:T(2,128)}, u32[]{:S(2)}) copy-start(s32[128,2]{0,1:T(2,128)} %param.23) | copy-start | bytes 3076
  195.4 87.3 %all-gather.5.cloned.1.call-start = ((), (), s32[]{:S(2)}) async-start(), calls=%async_computation.4 | async-start | bytes 6488064 | tf_op jit(solution)/shard_map/all_gather | solution.py:127
  219.1 4.3 %copy-start.5 = (f32[6144]{0:T(1024)S(1)}, f32[6144]{0:T(1024)}, u32[]{:S(2)}) copy-start(f32[6144]{0:T(1024)} %param.22) | copy-start | bytes 73732
  222.3 1.1 copy-start.1
  235.7 151.2 %reduce-scatter.2.cloned.1.call-start = ((), (), s32[]{:S(2)}) async-start(), calls=%async_computation.5 | async-start | bytes 6488064 | tf_op jit(solution)/shard_map/reduce_scatter | solution.py:131
  301.5 91.4 %copy-start.4 = (f32[128,2]{0,1:T(2,128)S(1)}, f32[128,2]{0,1:T(2,128)}, u32[]{:S(2)}) copy-start(f32[128,2]{0,1:T(2,128)} %param.24) | copy-start | bytes 3076
  388.6 10.7 %all-to-all-start.2 = ((bf16[4,4,6144]{2,1,0:T(4,128)(2,1)}), bf16[4,4,6144]{2,1,0:T(4,128)(2,1)}, u32[]{:S(2)}, u32[]{:S(2)}) async-start(bf16[4,4,6144]{2,1,0:T(4,128)(2,1)} %reshape.116), calls=%async_computation.3 | async-start | bytes 393216 | tf_op jit(solution)/shard_map/all_to_all | solution.py:138
Sparse Core Ops, SparseCore 0:
  26.9 65.4 all-gather.6
  235.8 46.8 all-gather.4
  301.6 85.2 reduce-scatter.1
where the time goes:
time: 411 us; the launch traced here: 409 us
  waiting for transfers between devices  186 us (45%)
  other arithmetic  88.4 us (22%)
  matrix products  44.2 us (11%)
  local copies, waits for them, and re-layouts  35.1 us (9%)
  blocking collectives  32.2 us (8%)
  between operations  13.9 us (3%)
  starting transfers between devices  8.89 us (2%)
    reduce_scatter x1, waiting for transfers between devices, local(): lax.psum_scatter(jnp.dot(activations, down_matrix, preferred_element_type...  85.5 us
    select_n x32, other arithmetic, turn(): return jax.tree.map(lambda a, b: jnp.where(reached, a, b), new, before)  72.5 us
    all_gather x1, waiting for transfers between devices, local(): pieces = lax.all_gather(flat_rows, 'ctx', axis=0, tiled=True)  47 us
    all_gather x1, waiting for transfers between devices, entering(): lax.all_gather(part.astype(kind), axis)  38.4 us
    all_gather x1, blocking collectives, entering(): lax.all_gather(part.astype(kind), axis)  22.8 us
    unnamed x21, local copies, waits for them, and re-layouts  17.3 us
    dot_general x1, matrix products, local(): jnp.dot(activations, down_matrix, preferred_element_type=jnp.float32)  12.1 us
    all_to_all x1, waiting for transfers between devices, local(): lax.all_to_all(attention, 'exp', split_axis=0, concat_axis=1, tiled=True)  11.3 us
  transfers between devices with their start and end apart: 5, of which 5 were waited for; matrix products, arithmetic and copies ran while one was open for 4% of the time, Pallas kernels for 0%

commit v1 on v0

--- a/solution.py
+++ b/solution.py
@@ -124,7 +124,9 @@
     gate_matrix = w_gate[0]
     up_matrix = w_up[0]
     down_matrix = w_down[0]
-    pieces = lax.all_gather(flat_rows, "ctx", axis=0, tiled=True)
+    pieces = jnp.concatenate(
+        jax.lax.all_to_all(jnp.stack(jax.lax.axis_size("ctx") * [flat_rows]), "ctx", 0, 0), axis=0
+    )
     gate_part = jnp.dot(pieces, gate_matrix, preferred_element_type=jnp.float32)
     up_part = jnp.dot(pieces, up_matrix, preferred_element_type=jnp.float32)
     activations = (jax.nn.silu(gate_part) * up_part).astype(jnp.bfloat16)

time: 411 us -> 441 us (1.073)
  blocking collectives: 32.2 us -> 111 us
  waiting for transfers between devices: 186 us -> 137 us
    all_to_all x0 -> x1, blocking collectives: none -> 79 us  [local(): jax.lax.all_to_all(jnp.stack(jax.lax.axis_size('ctx') * [flat_rows]), 'ct...]
    all_gather x1 -> x0, waiting for transfers between devices: 47 us -> none  [local(): pieces = lax.all_gather(flat_rows, 'ctx', axis=0, tiled=True)]
    unnamed x21 -> x25, local copies, waits for them, and re-layouts: 17.3 us -> 19.9 us
  transfers between devices with their start and end apart: 5 -> 4, of which waited for: 5 -> 4; matrix products, arithmetic and copies ran while one was open for 4% -> 4% of each run, Pallas kernels for 0% -> 0%
where the time goes in v1:
time: 441 us; the launch traced here: 439 us
  waiting for transfers between devices  137 us (31%)
  blocking collectives  111 us (25%)
  other arithmetic  88.4 us (20%)
  matrix products  40.3 us (9%)
  local copies, waits for them, and re-layouts  39.4 us (9%)
  between operations  14.2 us (3%)
  starting transfers between devices  8.88 us (2%)
    reduce_scatter x1, waiting for transfers between devices, local(): lax.psum_scatter(jnp.dot(activations, down_matrix, preferred_element_type...  83.3 us
    all_to_all x1, blocking collectives, local(): jax.lax.all_to_all(jnp.stack(jax.lax.axis_size('ctx') * [flat_rows]), 'ct...  79 us
    select_n x32, other arithmetic, turn(): return jax.tree.map(lambda a, b: jnp.where(reached, a, b), new, before)  72.5 us
    all_gather x1, waiting for transfers between devices, entering(): lax.all_gather(part.astype(kind), axis)  38.4 us
    all_gather x1, blocking collectives, entering(): lax.all_gather(part.astype(kind), axis)  22.8 us
    unnamed x25, local copies, waits for them, and re-layouts  19.9 us
    dot_general x1, matrix products, local(): jnp.dot(activations, down_matrix, preferred_element_type=jnp.float32)  12.1 us
    all_to_all x1, waiting for transfers between devices, local(): lax.all_to_all(attention, 'exp', split_axis=0, concat_axis=1, tiled=True)  11.3 us
  transfers between devices with their start and end apart: 4, of which 4 were waited for; matrix products, arithmetic and copies ran while one was open for 4% of the time, Pallas kernels for 0%

profile of v1, /device:TPU:0, one launch (start us, length us, event | category | flops | bytes accessed | tf_op | source)
XLA Modules:
  0.0 439.3 jit_solution(16828029567589078754)
XLA Ops:
  10.1 3.1 reduce-window.6
  15.9 2.6 copy.101
  18.5 2.6 copy.106
  22.4 4.3 fusion.35
  27.7 22.8 %all-gather.1 = bf16[32,1,12]{2,1,0:T(2,128)(2,1)S(1)} all-gather(bf16[1,1,12]{2,1,0:T(2,128)(2,1)S(1)} %bitcast.101), channel_id=1, replica_groups=mesh['ctx'=32,'exp'=4] {'ctx'}, dimensions={0}, use_global_device_ids=true | all-gather | bytes 792 | tf_op jit(solution)/shard_map/all_gather | solution.py:13
  50.5 2.6 copy.100
  53.9 38.4 %all-gather.4.cloned.1.call-done = bf16[384,128,128]{2,1,0:T(8,128)(2,1)} async-done(((bf16[12,128,128]{2,1,0:T(8,128)(2,1)}), bf16[384,128,128]{2,1,0:T(8,128)(2,1)}) %all-gather.4.cloned.1.call-update) | async-done | bytes 12582928 | tf_op jit(solution)/shard_map/all_gather | solution.py:13
  92.4 72.8 %while.18 = (s32[]{:T(128)}, f32[12,128,128]{2,1,0:T(8,128)}, s32[]{:T(128)}, bf16[32,12]{1,0:T(8,128)(2,1)S(1)}, bf16[32,12,128,128]{3,2,1,0:T(8,128)(2,1)}, /*index=5*/s32[]{:T(128)}, s32[]{:T(128)}) while((s32[]{:T(128)}, f32[12,128,128]{2,1,0:T(8,128)}, s32[]{:T(128)}, bf16[32,12]{1,0:T(8,128)(2,1)S(1)}, ...), condition=%wide.region_3.4_spmd.clone, body=%wide.region_2.3_spmd.clone.sunk | while | flops 983056 | bytes 1966305 | solution.py:30
  165.1 8.3 %fusion.20 = f32[12,128,512]{1,2,0:T(8,128)} fusion(f32[12,128,128]{2,1,0:T(8,128)} %get-tuple-element.117, bf16[512,12,128]{0,2,1:T(8,128)(2,1)} %bitcast.90, f32[512,12]{0,1:T(8,128)} %get-tuple-element.174), kind=kOutput, calls=%fused_computation.30 | convolution fusion | flops 1209532416 | bytes 5529600 | tf_op jit(solution)/shard_map/while/body/eval_jaxpr/thd,hde->the/dot_general | solution.py:89
  173.4 8.8 %fusion.19 = bf16[512,12,128]{2,0,1:T(8,128)(2,1)} fusion(f32[12,128,512]{1,2,0:T(8,128)} %fusion.20, bf16[512,12,128]{0,2,1:T(8,128)(2,1)} %bitcast.89, f32[12,512]{1,0:T(8,128)} %bitcast.96, pred[512,512]{1,0:T(8,128)(4,1)} %iota_compare_fusion, bf16[512,12,128]{0,2,1:T(8,128)(2,1)} %bitcast.91, bf16[512,12,128]{0,2,1:T(8,128)(2,1)} %bitcast.87), kind=kOutput, calls=%fused_computation.28 | convolution fusion | flops 1627914240 | bytes 9723904 | tf_op jit(solution)/shard_map/while/body/eval_jaxpr/hts,shd->thd/dot_general | solution.py:85
  184.8 3.5 all_to_all.19
  188.3 2.8 copy.115
  191.1 4.3 all-to-all-start
  205.6 11.3 %all-to-all-done = bf16[4,128,1536]{1,2,0:T(8,128)(2,1)} async-done(((bf16[4,128,1536]{1,2,0:T(8,128)(2,1)}), bf16[4,128,1536]{1,2,0:T(8,128)(2,1)}, u32[]{:S(2)}, u32[]{:S(2)}) %all-to-all-start) | async-done | bytes 1572896 | tf_op jit(solution)/shard_map/all_to_all | solution.py:94
  219.1 3.2 fusion.12
  224.7 9.4 %all_to_all.28 = bf16[4,4,6144]{2,1,0:T(4,128)(2,1)} all-to-all(bf16[4,4,6144]{2,1,0:T(4,128)(2,1)S(1)} %convolution_convert_fusion.1), channel_id=1, replica_groups=mesh['ctx'=32,'exp'=4] {'exp'}, dimensions={0} | all-to-all | bytes 393216 | tf_op jit(solution)/shard_map/all_to_all | solution.py:122
  237.4 79.0 %all_to_all.29 = bf16[32,16,6144]{2,1,0:T(8,128)(2,1)S(1)} all-to-all(bf16[32,16,6144]{2,1,0:T(8,128)(2,1)S(1)} %stack.3), channel_id=1, replica_groups=mesh['ctx'=32,'exp'=4] {'ctx'}, dimensions={0} | all-to-all | bytes 12582912 | tf_op jit(solution)/shard_map/all_to_all | solution.py:128
  316.4 2.7 copy-done.1
  319.0 2.8 fusion.10
  321.9 12.1 %convolution_convert_fusion = bf16[512,6144]{1,0:T(8,128)(2,1)} fusion(bf16[1,288,6144]{2,1,0:T(8,128)(2,1)S(1)} %copy-done, bf16[512,6144]{1,0:T(8,128)(2,1)} %bitcast.85, bf16[1,6144,288]{1,2,0:T(8,128)(2,1)} %param.26, f32[512,288]{0,1:T(8,128)} %fusion.10), kind=kOutput, calls=%fused_computation.4 | convolution fusion | flops 3627909120 | bytes 20250624 | tf_op jit(solution)/shard_map/dot_general | solution.py:134
  334.0 83.3 %reduce-scatter.2.cloned.1.call-done = bf16[16,6144]{1,0:T(8,128)(2,1)} async-done(((bf16[512,6144]{1,0:T(8,128)(2,1)}), bf16[16,6144]{1,0:T(8,128)(2,1)}) %reduce-scatter.2.cloned.1.call-update) | async-done | bytes 196624 | tf_op jit(solution)/shard_map/reduce_scatter | solution.py:133
  418.9 4.3 all-to-all-start.3
  425.8 3.8 all-to-all-done.3
  429.6 2.8 fusion.2
  (117 shorter events, 106.2 us)
Async XLA Ops:
  7.2 314.7 %copy-start = (bf16[1,288,6144]{2,1,0:T(8,128)(2,1)S(1)}, bf16[1,288,6144]{2,1,0:T(8,128)(2,1)}, u32[]{:S(2)}) copy-start(bf16[1,288,6144]{2,1,0:T(8,128)(2,1)} %param.27) | copy-start | bytes 10616836
  7.2 85.2 %all-gather.4.cloned.1.call-start = ((), (), s32[]{:S(2)}) async-start(), calls=%async_computation.6 | async-start | bytes 12976128 | tf_op jit(solution)/shard_map/all_gather | solution.py:13
  15.1 0.6 copy-start.3
  191.1 25.8 %all-to-all-start = ((bf16[4,128,1536]{1,2,0:T(8,128)(2,1)}), bf16[4,128,1536]{1,2,0:T(8,128)(2,1)}, u32[]{:S(2)}, u32[]{:S(2)}) async-start(bf16[4,128,1536]{1,2,0:T(8,128)(2,1)} %copy.115), calls=%async_computation | async-start | bytes 3145728 | tf_op jit(solution)/shard_map/all_to_all | solution.py:94
  195.4 5.4 %copy-start.4 = (s32[128,2]{0,1:T(2,128)S(1)}, s32[128,2]{0,1:T(2,128)}, u32[]{:S(2)}) copy-start(s32[128,2]{0,1:T(2,128)} %param.23) | copy-start | bytes 3076
  195.4 221.8 %reduce-scatter.2.cloned.1.call-start = ((), (), s32[]{:S(2)}) async-start(), calls=%async_computation.5 | async-start | bytes 6488064 | tf_op jit(solution)/shard_map/reduce_scatter | solution.py:133
  219.1 4.3 copy-start.7
  222.3 1.1 copy-start.2
  237.4 81.7 %copy-start.6 = (bf16[1,6144,288]{1,2,0:T(8,128)(2,1)S(1)}, bf16[1,6144,288]{1,2,0:T(8,128)(2,1)}, u32[]{:S(2)}) copy-start(bf16[1,6144,288]{1,2,0:T(8,128)(2,1)} %param.25) | copy-start | bytes 10616836
  316.4 2.7 copy-start.1
  333.9 89.3 %copy-start.5 = (f32[128,2]{0,1:T(2,128)S(1)}, f32[128,2]{0,1:T(2,128)}, u32[]{:S(2)}) copy-start(f32[128,2]{0,1:T(2,128)} %param.24) | copy-start | bytes 3076
  418.9 10.7 %all-to-all-start.3 = ((bf16[4,4,6144]{2,1,0:T(4,128)(2,1)}), bf16[4,4,6144]{2,1,0:T(4,128)(2,1)}, u32[]{:S(2)}, u32[]{:S(2)}) async-start(bf16[4,4,6144]{2,1,0:T(4,128)(2,1)} %reshape.118), calls=%async_computation.4 | async-start | bytes 393216 | tf_op jit(solution)/shard_map/all_to_all | solution.py:140
Sparse Core Ops, SparseCore 0:
  26.9 65.4 all-gather.3
  334.1 83.1 reduce-scatter.1
